TPU v7x, 512 devices: a whole 4x4x16 slice. The times are simulated.
512 devices in a mesh: walk: 64 (over z, y), col: 8 (over x, core).
Axes of the slice: x: 4, y: 4, z: 16, core: 2. Of those that a mesh axis runs over, the one named last changes fastest.
Arguments:
- jacobian: float32 [384, 524288], P('walk', 'col'), may hold values from -25 to 25
- prev_update: float32 [8, 65536], P('col', 'walk'), may hold values from -6 to 6
- base_energy: float32 [384], P('walk'), may hold values from -6 to 6
- elec_pos: float32 [384, 3, 66], P('walk'), may hold values from -8 to 8
- atom_pos: float32 [3, 21], replicated, may hold values from -6 to 6
- quad_ratio: float32 [384, 21, 66, 12], P('walk'), may hold values from -1.2 to 1.2
- rotation: int32 [384, 66], P('walk'), may hold values from 0 to 15
- channels: int32 [21], replicated, may hold values from 1 to 3
- ecp_coef: float32 [21, 3], replicated, may hold values from 0.5 to 2
- ecp_expo: float32 [21, 3], replicated, may hold values from 0.2 to 2
Outputs:
- local_energy: float32 [384], P('walk')
- update: float32 [8, 65536], P('col', 'walk')
All inputs are finite; a program needn't handle non-finite values.
Results may differ from a plain program's by a relative error of at most 0.0003.
Values sent between devices are 32-bit elements; how exact they have to be, the bound alone decides.
No kernel may reach another device: no remote copies, remote signals or barrier semaphores. Data moves between devices by JAX's collectives and lax.ppermute only.
A program may use at most 64 MiB of HBM per device.

v0:
```python
import math
import jax
import jax.numpy as jnp
from jax import lax
from jax.sharding import PartitionSpec as P

NROT = 16
momentum = 0.9
damping = 0.1


def icosa_points():
    golden = (1.0 + math.sqrt(5.0)) / 2.0
    length = math.sqrt(1.0 + golden * golden)
    rows = []
    for first in (-1.0, 1.0):
        for second in (-golden, golden):
            rows.append((0.0, first / length, second / length))
            rows.append((first / length, second / length, 0.0))
            rows.append((second / length, 0.0, first / length))
    return jnp.asarray(rows, dtype=jnp.float32).T


def rotation_table(count):
    angle = jnp.arange(count, dtype=jnp.float32)
    turn_z = 2.0 * math.pi * angle / count
    turn_x = 0.9 * angle
    cz, sz = (jnp.cos(turn_z), jnp.sin(turn_z))
    cx, sx = (jnp.cos(turn_x), jnp.sin(turn_x))
    zeros = jnp.zeros_like(cz)
    matrix = jnp.stack(
        [
            jnp.stack([cz, -sz * cx, sz * sx], axis=-1),
            jnp.stack([sz, cz * cx, -cz * sx], axis=-1),
            jnp.stack([zeros, sx, cx], axis=-1),
        ],
        axis=1,
    )
    points = icosa_points()
    rotated = matrix[:, :, 0, None] * points[None, 0, :]
    rotated = rotated + matrix[:, :, 1, None] * points[None, 1, :]
    rotated = rotated + matrix[:, :, 2, None] * points[None, 2, :]
    return rotated.reshape(count, -1)


def nonlocal_energy(elec_pos, atom_pos, quad_ratio, rotation, channels, ecp_coef, ecp_expo):
    walkers, electrons = rotation.shape
    count = NROT
    table = rotation_table(count)
    onehot = (rotation[:, :, None] == jnp.arange(count, dtype=jnp.int32)[None, None, :]).astype(
        jnp.float32
    )
    rotated = jnp.einsum("wek,kf->wef", onehot, table, precision=lax.Precision.HIGHEST)
    rotated = rotated.reshape(walkers, electrons, 3, -1)
    diff = elec_pos[:, :, None, :] - atom_pos[None, :, :, None]
    dist2 = jnp.sum(diff * diff, axis=1)
    unit = diff / jnp.sqrt(dist2 + 0.01)[:, None, :, :]
    cosang = unit[:, 0, :, :, None] * rotated[:, None, :, 0, :]
    cosang = cosang + unit[:, 1, :, :, None] * rotated[:, None, :, 1, :]
    cosang = cosang + unit[:, 2, :, :, None] * rotated[:, None, :, 2, :]
    quad = quad_ratio.shape[-1]
    lmax = ecp_coef.shape[1]
    lower = jnp.ones_like(cosang)
    upper = cosang
    total = jnp.zeros((walkers,), jnp.float32)
    for level in range(lmax):
        if level == 0:
            poly = lower
        elif level == 1:
            poly = upper
        else:
            fresh = ((2 * level - 1) * cosang * upper - (level - 1) * lower) / level
            lower, upper = (upper, fresh)
            poly = fresh
        angular = jnp.sum(poly * quad_ratio, axis=-1) / quad
        active = (channels > level).astype(jnp.float32)
        radial = ecp_coef[None, :, level, None] * jnp.exp(-ecp_expo[None, :, level, None] * dist2)
        term = (2 * level + 1) * active[None, :, None] * radial * angular
        total = total + jnp.sum(term, axis=(1, 2))
    return total


def sum_pieces(first, second):
    first_sum, second_sum = lax.psum((first, second), ("walk", "col"))
    return (first_sum, second_sum)


def body(
    jacobian,
    prev_update,
    base_energy,
    elec_pos,
    atom_pos,
    quad_ratio,
    rotation,
    channels,
    ecp_coef,
    ecp_expo,
):
    energy_mine = base_energy + nonlocal_energy(
        elec_pos, atom_pos, quad_ratio, rotation, channels, ecp_coef, ecp_expo
    )
    columns = lax.all_to_all(jacobian, "walk", split_axis=1, concat_axis=0, tiled=True)
    walkers = columns.shape[0]
    params_total = columns.shape[1] * lax.axis_size("walk") * lax.axis_size("col")
    scale = 1.0 / params_total
    centred = columns - jnp.mean(columns, axis=0, keepdims=True)
    prev_mine = prev_update[0]
    gram_part = (
        jnp.dot(
            centred, centred.T, precision=lax.Precision.HIGHEST, preferred_element_type=jnp.float32
        )
        * scale
    )
    along_part = (
        jnp.dot(
            centred, prev_mine, precision=lax.Precision.HIGHEST, preferred_element_type=jnp.float32
        )
        * scale
    )
    extra = along_part[:, None]
    gram, extra_sum = sum_pieces(gram_part, extra)
    along = extra_sum[:, 0]
    energies = lax.all_gather(energy_mine, "walk", axis=0, tiled=True)
    eps = -(energies - jnp.mean(energies)) / math.sqrt(walkers)
    system = gram + damping * jnp.eye(walkers, dtype=jnp.float32)
    factor = jnp.linalg.cholesky(system)
    solved = jax.scipy.linalg.cho_solve((factor, True), eps - momentum * along)
    update_mine = (
        jnp.dot(
            solved, centred, precision=lax.Precision.HIGHEST, preferred_element_type=jnp.float32
        )
        + momentum * prev_mine
    )
    return (energy_mine, update_mine[None, :])


def solution(mesh):
    in_specs = (
        P("walk", "col"),
        P("col", "walk"),
        P("walk"),
        P("walk", None, None),
        P(),
        P("walk", None, None, None),
        P("walk", None),
        P(),
        P(),
        P(),
    )
    out_specs = (P("walk"), P("col", "walk"))
    return jax.shard_map(body, mesh=mesh, in_specs=in_specs, out_specs=out_specs, check_vma=False)
```

profile of v0, /device:TPU:1, one launch (start us, length us, event | category | flops | bytes accessed | tf_op | source)
XLA Modules:
  0.0 826.4 jit_solution(6028116304954348564)
XLA Ops:
  7.3 19.4 %all-to-all-start = ((f32[6,64,1024]{2,0,1:T(8,128)}), f32[6,64,1024]{2,0,1:T(8,128)S(1)}, u32[]{:S(2)}, u32[]{:S(2)}) async-start(f32[6,64,1024]{2,0,1:T(8,128)} %bitcast.162), calls=%async_computation | async-start | bytes 4194304 | tf_op jit(solution)/shard_map/all_to_all | solution.py:103
  28.4 1.3 dynamic-slice.3
  32.3 187.9 %all-reduce.1 = f32[384]{0:T(512)S(1)} all-reduce(f32[384]{0:T(512)S(1)} %get-tuple-element.32), channel_id=1, replica_groups=mesh['walk'=64,'col'=8] {'walk'}, use_global_device_ids=true, to_apply=%add.1 | all-reduce | flops 384 | bytes 3072
  221.7 1.6 subtract_bitcast_fusion
  223.3 1.6 sub.49
  225.0 3.4 convolution_multiply_fusion
  228.4 1.4 convolution_reduce_fusion
  229.9 133.3 %psum.15 = f32[384,1]{0,1:T(1,128)S(1)} all-reduce(f32[384,1]{0,1:T(1,128)S(1)} %broadcast_in_dim.6), channel_id=1, replica_groups=mesh['walk'=64,'col'=8] {'walk','col'}, use_global_device_ids=true, to_apply=%region_16.17 | all-reduce | flops 384 | bytes 3072 | tf_op jit(solution)/shard_map/psum | solution.py:84
  363.3 355.0 %all-reduce.4.cloned.1.call-done = f32[384,384]{0,1:T(8,128)} async-done(((f32[384,384]{0,1:T(8,128)}), f32[384,384]{0,1:T(8,128)}) %all-reduce.4.cloned.1.call-update) | async-done | bytes 589840 | tf_op jit(solution)/shard_map/psum | solution.py:84
  718.2 1.2 select_add_fusion
  719.8 11.7 %cholesky.76 = f32[128,128]{1,0:T(8,128)S(1)} custom-call(f32[128,128]{1,0:T(8,128)S(1)} %cholesky.189), custom_call_target="Cholesky" | custom-call | tf_op jit(solution)/shard_map/jit(cholesky)/cholesky | solution.py:127
  731.5 9.8 %custom-call.26 = f32[1,128,128]{1,2,0:T(8,128)S(1)} custom-call(f32[1,128,128]{2,1,0:T(8,128)S(1)} %get-tuple-element.45), custom_call_target="InvertDiagBlocksLowerTriangular" | custom-call | tf_op jit(solution)/shard_map/jit(cholesky)/cholesky | solution.py:127
  742.1 11.7 %cholesky.160 = f32[128,128]{1,0:T(8,128)S(1)} custom-call(f32[128,128]{1,0:T(8,128)S(1)} %cholesky.193), custom_call_target="Cholesky" | custom-call | tf_op jit(solution)/shard_map/jit(cholesky)/cholesky | solution.py:127
  754.0 10.0 %custom-call.27 = f32[1,128,128]{1,2,0:T(8,128)S(1)} custom-call(f32[1,128,128]{2,1,0:T(8,128)S(1)} %get-tuple-element.43), custom_call_target="InvertDiagBlocksLowerTriangular" | custom-call | tf_op jit(solution)/shard_map/jit(cholesky)/cholesky | solution.py:127
  764.7 11.7 %cholesky.179 = f32[128,128]{1,0:T(8,128)S(1)} custom-call(f32[128,128]{1,0:T(8,128)S(1)} %convolution_subtract_fusion.1), custom_call_target="Cholesky" | custom-call | tf_op jit(solution)/shard_map/jit(cholesky)/cholesky | solution.py:127
  776.6 0.7 compare_reduce_fusion
  777.3 0.6 compare_reduce_fusion.1
  779.9 6.7 while.1
  780.6 1.4 dynamic-slice.8
  782.8 1.4 dynamic-slice.8
  785.0 1.4 dynamic-slice.8
  786.6 29.5 %custom-call.28 = f32[3,128,128]{1,2,0:T(8,128)S(1)} custom-call(f32[3,128,128]{2,1,0:T(8,128)S(1)} %get-tuple-element.9), custom_call_target="InvertDiagBlocksLowerTriangular" | custom-call | tf_op jit(solution)/shard_map/jit(_cho_solve)/triangular_solve | solution.py:128
  818.0 0.9 fusion.33
  818.9 0.6 multiply_add_fusion.1
  (123 shorter events, 10.7 us)
Async XLA Ops:
  7.2 20.8 %copy-start.11 = (f32[12]{0:T(128)S(1)}, f32[12]{0:T(128)}, u32[]{:S(2)}) copy-start(f32[12]{0:T(128)} %constant.198) | copy-start | bytes 148
  7.2 20.9 %copy-start.10 = (f32[12]{0:T(128)S(1)}, f32[12]{0:T(128)}, u32[]{:S(2)}) copy-start(f32[12]{0:T(128)} %constant.200) | copy-start | bytes 148
  7.2 20.9 %copy-start.9 = (f32[12]{0:T(128)S(1)}, f32[12]{0:T(128)}, u32[]{:S(2)}) copy-start(f32[12]{0:T(128)} %constant.202) | copy-start | bytes 148
  7.2 21.2 %copy-start.3 = (f32[6,3,66]{2,1,0:T(4,128)S(1)}, f32[6,3,66]{2,1,0:T(4,128)}, u32[]{:S(2)}) copy-start(f32[6,3,66]{2,1,0:T(4,128)} %param.14) | copy-start | bytes 14260
  7.2 23.1 %copy-start.4 = (f32[3,21]{1,0:T(4,128)S(1)}, f32[3,21]{1,0:T(4,128)}, u32[]{:S(2)}) copy-start(f32[3,21]{1,0:T(4,128)} %param.15) | copy-start | bytes 760
  7.2 23.2 %copy-start.12 = (s32[21]{0:T(128)S(1)}, s32[21]{0:T(128)}, u32[]{:S(2)}) copy-start(s32[21]{0:T(128)} %param.18) | copy-start | bytes 256
  7.2 23.3 %copy-start.6 = (f32[21,3]{0,1:T(4,128)S(1)}, f32[21,3]{0,1:T(4,128)}, u32[]{:S(2)}) copy-start(f32[21,3]{0,1:T(4,128)} %param.20) | copy-start | bytes 760
  7.2 23.3 %copy-start.7 = (f32[21,3]{0,1:T(4,128)S(1)}, f32[21,3]{0,1:T(4,128)}, u32[]{:S(2)}) copy-start(f32[21,3]{0,1:T(4,128)} %param.19) | copy-start | bytes 760
  7.3 23.3 %copy-start.5 = (s32[6,66]{1,0:T(8,128)S(1)}, s32[6,66]{1,0:T(8,128)}, u32[]{:S(2)}) copy-start(s32[6,66]{1,0:T(8,128)} %param.17) | copy-start | bytes 4756
  7.3 214.3 %all-to-all-start = ((f32[6,64,1024]{2,0,1:T(8,128)}), f32[6,64,1024]{2,0,1:T(8,128)S(1)}, u32[]{:S(2)}, u32[]{:S(2)}) async-start(f32[6,64,1024]{2,0,1:T(8,128)} %bitcast.162), calls=%async_computation | async-start | bytes 4194304 | tf_op jit(solution)/shard_map/all_to_all | solution.py:103
  26.7 4.2 copy-start.1
  26.7 691.5 %all-reduce.4.cloned.1.call-start = ((), (), s32[]{:S(2)}) async-start(), calls=%async_computation.1 | async-start | bytes 1179648 | tf_op jit(solution)/shard_map/psum | solution.py:84
  30.5 1.2 copy-start.8
  225.0 3.5 copy-start.2
  718.2 1.4 copy-start
Sparse Core Ops, SparseCore 0:
  228.5 489.6 all-reduce.3
where the time goes:
time: 827 us; the launch traced here: 826 us
  waiting for transfers between devices  355 us (43%)
  blocking collectives  321 us (39%)
  other arithmetic  92.2 us (11%)
  starting transfers between devices  19.5 us (2%)
  between operations  17.8 us (2%)
  local copies, waits for them, and re-layouts  11.5 us (1%)
  matrix products  9.1 us (1%)
    psum x1, waiting for transfers between devices, sum_pieces(): first_sum, second_sum = lax.psum((first, second), ('walk', 'col'))  355 us
    unnamed x1, blocking collectives  188 us
    psum x1, blocking collectives, sum_pieces(): first_sum, second_sum = lax.psum((first, second), ('walk', 'col'))  133 us
    another operation x10, other arithmetic, body(): factor = jnp.linalg.cholesky(system)  56.4 us
    another operation x3, other arithmetic, body(): solved = jax.scipy.linalg.cho_solve((factor, True), eps - momentum * along)  29.5 us
    all_to_all x1, starting transfers between devices, body(): lax.all_to_all(jacobian, 'walk', split_axis=1, concat_axis=0, tiled=True)  19.4 us
  transfers between devices with their start and end apart: 2, of which 1 were waited for; matrix products, arithmetic and copies ran while one was open for 1% of the time, Pallas kernels for 0%

commit v1 on v0

--- a/solution.py
+++ b/solution.py
@@ -81,7 +81,12 @@
 
 
 def sum_pieces(first, second):
-    first_sum, second_sum = lax.psum((first, second), ("walk", "col"))
+
+    def group_the_values(v0):
+        carry_out = jax.lax.psum(jax.lax.psum(v0, axis_name="walk"), axis_name="col")
+        return carry_out
+
+    first_sum, second_sum = group_the_values((first, second))
     return (first_sum, second_sum)
 
 

time: 827 us -> 576 us (0.70)
  blocking collectives: 321 us -> 158 us
  waiting for transfers between devices: 355 us -> 264 us
    unnamed x1 -> x0, blocking collectives: 188 us -> none
    psum x1 -> x2, waiting for transfers between devices: 355 us -> 174 us  [the longest x1 92.3 us: group_the_values(): jax.lax.psum(v0, axis_name='walk')]
    all_to_all x1, waiting for transfers between devices: 0.01 us -> 89.8 us  [body(): lax.all_to_all(jacobian, 'walk', split_axis=1, concat_axis=0, tiled=True)]
    psum x1 -> x2, blocking collectives: 133 us -> 158 us  [the longest x1 114 us: group_the_values(): jax.lax.psum(v0, axis_name='walk')]
  transfers between devices with their start and end apart: 2 -> 3, of which waited for: 1 -> 3; matrix products, arithmetic and copies ran while one was open for 1% -> 1% of each run, Pallas kernels for 0% -> 0%
where the time goes in v1:
time: 576 us; the launch traced here: 575 us
  waiting for transfers between devices  264 us (46%)
  blocking collectives  158 us (27%)
  other arithmetic  93 us (16%)
  starting transfers between devices  19.5 us (3%)
  between operations  17.8 us (3%)
  local copies, waits for them, and re-layouts  13.3 us (2%)
  matrix products  9.1 us (2%)
    psum x1, blocking collectives, group_the_values(): jax.lax.psum(v0, axis_name='walk')  114 us
    psum x1, waiting for transfers between devices, group_the_values(): jax.lax.psum(v0, axis_name='walk')  92.3 us
    all_to_all x1, waiting for transfers between devices, body(): lax.all_to_all(jacobian, 'walk', split_axis=1, concat_axis=0, tiled=True)  89.8 us
    psum x1, waiting for transfers between devices, group_the_values(): jax.lax.psum(jax.lax.psum(v0, axis_name='walk'), axis_name='col')  82.1 us
    another operation x10, other arithmetic, body(): factor = jnp.linalg.cholesky(system)  56.4 us
    psum x1, blocking collectives, group_the_values(): jax.lax.psum(jax.lax.psum(v0, axis_name='walk'), axis_name='col')  44 us
    another operation x3, other arithmetic, body(): solved = jax.scipy.linalg.cho_solve((factor, True), eps - momentum * along)  30.4 us
    all_to_all x1, starting transfers between devices, body(): lax.all_to_all(jacobian, 'walk', split_axis=1, concat_axis=0, tiled=True)  19.4 us
  transfers between devices with their start and end apart: 3, of which 3 were waited for; matrix products, arithmetic and copies ran while one was open for 1% of the time, Pallas kernels for 0%

profile of v1, /device:TPU:1, one launch (start us, length us, event | category | flops | bytes accessed | tf_op | source)
XLA Modules:
  0.0 574.7 jit_solution(9547280777765200089)
XLA Ops:
  7.3 19.4 %all-to-all-start = ((f32[6,64,1024]{2,0,1:T(8,128)}), f32[6,64,1024]{2,0,1:T(8,128)S(1)}, u32[]{:S(2)}, u32[]{:S(2)}) async-start(f32[6,64,1024]{2,0,1:T(8,128)} %bitcast.162), calls=%async_computation | async-start | bytes 4194304 | tf_op jit(solution)/shard_map/all_to_all | solution.py:108
  28.4 1.3 dynamic-slice.3
  31.8 89.8 %all-to-all-done = f32[6,64,1024]{2,0,1:T(8,128)S(1)} async-done(((f32[6,64,1024]{2,0,1:T(8,128)}), f32[6,64,1024]{2,0,1:T(8,128)S(1)}, u32[]{:S(2)}, u32[]{:S(2)}) %all-to-all-start) | async-done | bytes 1572896 | tf_op jit(solution)/shard_map/all_to_all | solution.py:108
  121.7 1.6 subtract_bitcast_fusion
  123.3 1.6 sub.49
  125.0 3.4 convolution_multiply_fusion
  129.1 1.4 convolution_reduce_fusion
  130.5 113.8 %all-reduce.2 = (f32[384,1]{0,1:T(1,128)S(1)}, f32[384]{0:T(512)S(1)}) all-reduce(f32[384,1]{0,1:T(1,128)S(1)} %broadcast_in_dim.6, f32[384]{0:T(512)S(1)} %get-tuple-element.34), channel_id=1, replica_groups=mesh['walk'=64,'col'=8] {'walk'}, use_global_device_ids=true, to_apply=%region_17.18 | all-reduce | flops 768 | bytes 6144 | tf_op jit(solution)/shard_map/psum | solution.py:86
  245.5 44.0 %psum.31 = f32[384,1]{0,1:T(1,128)S(1)} all-reduce(f32[384,1]{0,1:T(1,128)S(1)} %get-tuple-element.32), channel_id=1, replica_groups=mesh['walk'=64,'col'=8] {'col'}, use_global_device_ids=true, to_apply=%region_18.19 | all-reduce | flops 384 | bytes 3072 | tf_op jit(solution)/shard_map/psum | solution.py:86
  289.5 92.3 %all-reduce.6.cloned.1.call-done = f32[384,384]{0,1:T(8,128)} async-done(((f32[384,384]{0,1:T(8,128)}), f32[384,384]{0,1:T(8,128)}) %all-reduce.6.cloned.1.call-update) | async-done | bytes 589840 | tf_op jit(solution)/shard_map/psum | solution.py:86
  381.9 82.1 %all-reduce.8.cloned.1.call-done = f32[384,384]{0,1:T(8,128)} async-done(((f32[384,384]{0,1:T(8,128)}), f32[384,384]{0,1:T(8,128)}) %all-reduce.8.cloned.1.call-update) | async-done | bytes 589840 | tf_op jit(solution)/shard_map/psum | solution.py:86
  464.0 1.2 select_add_fusion
  465.5 11.7 %cholesky.76 = f32[128,128]{1,0:T(8,128)S(1)} custom-call(f32[128,128]{1,0:T(8,128)S(1)} %cholesky.189), custom_call_target="Cholesky" | custom-call | tf_op jit(solution)/shard_map/jit(cholesky)/cholesky | solution.py:132
  477.3 9.8 %custom-call.26 = f32[1,128,128]{1,2,0:T(8,128)S(1)} custom-call(f32[1,128,128]{2,1,0:T(8,128)S(1)} %get-tuple-element.47), custom_call_target="InvertDiagBlocksLowerTriangular" | custom-call | tf_op jit(solution)/shard_map/jit(cholesky)/cholesky | solution.py:132
  487.9 11.7 %cholesky.160 = f32[128,128]{1,0:T(8,128)S(1)} custom-call(f32[128,128]{1,0:T(8,128)S(1)} %cholesky.193), custom_call_target="Cholesky" | custom-call | tf_op jit(solution)/shard_map/jit(cholesky)/cholesky | solution.py:132
  499.8 10.0 %custom-call.27 = f32[1,128,128]{1,2,0:T(8,128)S(1)} custom-call(f32[1,128,128]{2,1,0:T(8,128)S(1)} %get-tuple-element.45), custom_call_target="InvertDiagBlocksLowerTriangular" | custom-call | tf_op jit(solution)/shard_map/jit(cholesky)/cholesky | solution.py:132
  510.5 11.7 %cholesky.179 = f32[128,128]{1,0:T(8,128)S(1)} custom-call(f32[128,128]{1,0:T(8,128)S(1)} %convolution_subtract_fusion.1), custom_call_target="Cholesky" | custom-call | tf_op jit(solution)/shard_map/jit(cholesky)/cholesky | solution.py:132
  522.3 0.7 compare_reduce_fusion
  525.7 8.5 %while.1 = (s32[]{:T(128)}, f32[384,384]{0,1:T(8,128)S(1)}, s32[3,2]{0,1:T(2,128)S(1)}, f32[3,128,128]{2,1,0:T(8,128)}, s32[]{:T(128)}) while((s32[]{:T(128)}, f32[384,384]{0,1:T(8,128)S(1)}, s32[3,2]{0,1:T(2,128)S(1)}, f32[3,128,128]{2,1,0:T(8,128)}, s32[]{:T(128)}) %tuple.50), condition=%wide.while_cond, body=%wide.while_body.sunk | while | flops 2 | bytes 393829 | solution.py:133
  526.3 1.4 dynamic-slice.8
  529.2 1.4 dynamic-slice.8
  532.0 1.4 dynamic-slice.8
  534.1 30.3 %custom-call.28 = f32[3,128,128]{1,2,0:T(8,128)S(1)} custom-call(f32[3,128,128]{2,1,0:T(8,128)} %get-tuple-element.9), custom_call_target="InvertDiagBlocksLowerTriangular" | custom-call | tf_op jit(solution)/shard_map/jit(_cho_solve)/triangular_solve | solution.py:133
  566.4 0.9 fusion.33
  (126 shorter events, 13.8 us)
Async XLA Ops:
  7.2 20.8 %copy-start.11 = (f32[12]{0:T(128)S(1)}, f32[12]{0:T(128)}, u32[]{:S(2)}) copy-start(f32[12]{0:T(128)} %constant.198) | copy-start | bytes 148
  7.2 20.9 %copy-start.10 = (f32[12]{0:T(128)S(1)}, f32[12]{0:T(128)}, u32[]{:S(2)}) copy-start(f32[12]{0:T(128)} %constant.200) | copy-start | bytes 148
  7.2 20.9 %copy-start.9 = (f32[12]{0:T(128)S(1)}, f32[12]{0:T(128)}, u32[]{:S(2)}) copy-start(f32[12]{0:T(128)} %constant.202) | copy-start | bytes 148
  7.2 21.2 %copy-start.3 = (f32[6,3,66]{2,1,0:T(4,128)S(1)}, f32[6,3,66]{2,1,0:T(4,128)}, u32[]{:S(2)}) copy-start(f32[6,3,66]{2,1,0:T(4,128)} %param.14) | copy-start | bytes 14260
  7.2 23.1 %copy-start.4 = (f32[3,21]{1,0:T(4,128)S(1)}, f32[3,21]{1,0:T(4,128)}, u32[]{:S(2)}) copy-start(f32[3,21]{1,0:T(4,128)} %param.15) | copy-start | bytes 760
  7.2 23.2 %copy-start.12 = (s32[21]{0:T(128)S(1)}, s32[21]{0:T(128)}, u32[]{:S(2)}) copy-start(s32[21]{0:T(128)} %param.18) | copy-start | bytes 256
  7.2 23.3 %copy-start.6 = (f32[21,3]{0,1:T(4,128)S(1)}, f32[21,3]{0,1:T(4,128)}, u32[]{:S(2)}) copy-start(f32[21,3]{0,1:T(4,128)} %param.20) | copy-start | bytes 760
  7.2 23.3 %copy-start.7 = (f32[21,3]{0,1:T(4,128)S(1)}, f32[21,3]{0,1:T(4,128)}, u32[]{:S(2)}) copy-start(f32[21,3]{0,1:T(4,128)} %param.19) | copy-start | bytes 760
  7.3 23.3 %copy-start.5 = (s32[6,66]{1,0:T(8,128)S(1)}, s32[6,66]{1,0:T(8,128)}, u32[]{:S(2)}) copy-start(s32[6,66]{1,0:T(8,128)} %param.17) | copy-start | bytes 4756
  7.3 114.3 %all-to-all-start = ((f32[6,64,1024]{2,0,1:T(8,128)}), f32[6,64,1024]{2,0,1:T(8,128)S(1)}, u32[]{:S(2)}, u32[]{:S(2)}) async-start(f32[6,64,1024]{2,0,1:T(8,128)} %bitcast.162), calls=%async_computation | async-start | bytes 4194304 | tf_op jit(solution)/shard_map/all_to_all | solution.py:108
  26.7 4.2 copy-start.1
  26.7 355.1 %all-reduce.6.cloned.1.call-start = ((), (), s32[]{:S(2)}) async-start(), calls=%async_computation.1 | async-start | bytes 1179648 | tf_op jit(solution)/shard_map/psum | solution.py:86
  125.0 3.5 copy-start.8
  125.0 4.1 copy-start.2
  128.4 335.6 %all-reduce.8.cloned.1.call-start = ((), (), s32[]{:S(2)}) async-start(), calls=%async_computation.2 | async-start | bytes 1179648 | tf_op jit(solution)/shard_map/psum | solution.py:86
  464.0 1.4 copy-start
Sparse Core Ops, SparseCore 0:
  128.6 253.2 all-reduce.5
  384.3 79.6 all-reduce.7
